TPU v7x, 256 devices: a whole 4x4x8 slice. The times are simulated.
256 devices in a mesh: blk: 32 (over x_lo, z, core), tp: 8 (over x_hi, y).
Axes of the slice: x: 4 (x_hi: 2, x_lo: 2; x = x_hi * 2 + x_lo), y: 4, z: 8, core: 2. Of those that a mesh axis runs over, the one named last changes fastest.
Arguments:
- tokens: bfloat16 [8192, 8192], P('blk', 'tp'), may hold values from -6 to 6
- weight: bfloat16 [8192, 2048], P('tp'), may hold values from -0.0625 to 0.0625
- bank_a: bfloat16 [32, 8192, 32], P('blk', 'tp'), may hold values from -0.0625 to 0.0625
- bank_b: bfloat16 [32, 32, 1024], P('blk'), may hold values from -1.5 to 1.5
- tile_map: int32 [64, 1], P('blk'), may hold values from 0 to 31
- grad_out: bfloat16 [8192, 2048], P(('blk', 'tp')), may hold values from -6 to 6
Outputs:
- key_value_output: bfloat16 [8192, 2048], P(('blk', 'tp'))
- token_gradient: bfloat16 [8192, 8192], P('blk', 'tp')
- grad_a: float32 [32, 8192, 32], P('blk', 'tp')
- grad_b: float32 [32, 32, 1024], P('blk', None, 'tp')
Inputs may be any that keep to these rules, and one draw needn't show every extreme that they name: `tile_map`: every one of the 32 adapters is the adapter of at least one tile.
All inputs are finite; a program needn't handle non-finite values.
Results may differ from a plain program's by a relative error of at most 0.003.
Values may be sent and summed in bfloat16 or wider, within the bound.
A program may use at most 64 MiB of HBM per device.

v0:
```python
import jax
import jax.numpy as jnp
from jax import lax
from jax.sharding import PartitionSpec as P

adapter_scale = 0.5


def on_device(tokens, weight, bank_a, bank_b, tile_map, grad_out):
    f32, bf16 = (jnp.float32, jnp.bfloat16)
    tile_ids = tile_map[:, 0]
    rows, feats = tokens.shape
    tiles = tile_ids.shape[0]
    tile_rows = rows // tiles
    rank_two = bank_a.shape[2]
    rank_one = rank_two // 2
    kv_width = bank_b.shape[2]
    tp_count = lax.axis_size("tp")
    tp_id = lax.axis_index("tp")
    kv_dev = kv_width // tp_count
    col0 = tp_id * kv_dev
    b_cols = lax.dynamic_slice_in_dim(bank_b, col0, kv_dev, 2)
    all_b = lax.all_gather(b_cols, "blk", axis=0, tiled=True)
    all_a = lax.all_gather(bank_a, "blk", axis=0, tiled=True)
    grad_rows = lax.all_gather(grad_out, "tp", axis=0, tiled=True)
    fac_a = jnp.stack([all_a[tile_ids[t]] for t in range(tiles)])
    fac_b = jnp.stack([all_b[tile_ids[t]] for t in range(tiles)])
    tok_t = tokens.reshape(tiles, tile_rows, feats)
    g_t = grad_rows.reshape(tiles, tile_rows, 2 * kv_width)
    g_key = lax.dynamic_slice_in_dim(g_t, col0, kv_dev, 2)
    g_val = lax.dynamic_slice_in_dim(g_t, kv_width + col0, kv_dev, 2)
    act_part = jnp.einsum("tre,tek->trk", tok_t, fac_a, preferred_element_type=f32)
    grad_part = jnp.concatenate(
        [
            jnp.einsum("trc,tkc->trk", g_key, fac_b[:, :rank_one], preferred_element_type=f32),
            jnp.einsum("trc,tkc->trk", g_val, fac_b[:, rank_one:], preferred_element_type=f32),
        ],
        axis=2,
    )
    both = lax.psum(jnp.stack([act_part, grad_part]), "tp")
    rank_act = both[0].astype(bf16)
    rank_grad = both[1].astype(bf16)
    lora_key = jnp.einsum(
        "trk,tkc->trc", rank_act[:, :, :rank_one], fac_b[:, :rank_one], preferred_element_type=f32
    ).reshape(rows, kv_dev)
    lora_val = jnp.einsum(
        "trk,tkc->trc", rank_act[:, :, rank_one:], fac_b[:, rank_one:], preferred_element_type=f32
    ).reshape(rows, kv_dev)
    base = jnp.dot(tokens, weight, preferred_element_type=f32)
    base = lax.dynamic_update_slice_in_dim(
        base, lax.dynamic_slice_in_dim(base, col0, kv_dev, 1) + adapter_scale * lora_key, col0, 1
    )
    base = lax.dynamic_update_slice_in_dim(
        base,
        lax.dynamic_slice_in_dim(base, kv_width + col0, kv_dev, 1) + adapter_scale * lora_val,
        kv_width + col0,
        1,
    )
    key_value_output = lax.psum_scatter(base, "tp", scatter_dimension=0, tiled=True).astype(bf16)
    backward = jnp.dot(grad_rows, weight.T, preferred_element_type=f32)
    adapter_back = jnp.einsum("tru,tyu->try", rank_grad, fac_a, preferred_element_type=f32)
    token_gradient = (backward + adapter_scale * adapter_back.reshape(rows, feats)).astype(bf16)
    down_grad = adapter_scale * jnp.einsum(
        "tre,trk->tek", tok_t, rank_grad, preferred_element_type=f32
    )
    up_grad = adapter_scale * jnp.concatenate(
        [
            jnp.einsum(
                "trk,trc->tkc", rank_act[:, :, :rank_one], g_key, preferred_element_type=f32
            ),
            jnp.einsum(
                "trk,trc->tkc", rank_act[:, :, rank_one:], g_val, preferred_element_type=f32
            ),
        ],
        axis=1,
    )
    size_a = feats * rank_two
    flat = jnp.concatenate([down_grad.reshape(tiles, -1), up_grad.reshape(tiles, -1)], axis=1)
    adapters = bank_a.shape[0] * lax.axis_size("blk")
    one_hot = (tile_ids[:, None] == jnp.arange(adapters, dtype=jnp.int32)[None, :]).astype(f32)
    dense = jnp.dot(one_hot.T, flat, precision=lax.Precision.HIGHEST, preferred_element_type=f32)
    summed = lax.psum_scatter(
        dense.reshape(adapters, -1, 128), "blk", scatter_dimension=0, tiled=True
    ).reshape(bank_a.shape[0], -1)
    grad_a = summed[:, :size_a].reshape(bank_a.shape[0], feats, rank_two)
    grad_b = summed[:, size_a:].reshape(bank_a.shape[0], rank_two, kv_dev)
    return (key_value_output, token_gradient, grad_a, grad_b)


def solution(mesh):
    in_specs = (
        P("blk", "tp"),
        P("tp", None),
        P("blk", "tp", None),
        P("blk", None, None),
        P("blk", None),
        P(("blk", "tp"), None),
    )
    out_specs = (P(("blk", "tp"), None), P("blk", "tp"), P("blk", "tp", None), P("blk", None, "tp"))
    return jax.shard_map(
        on_device, mesh=mesh, in_specs=in_specs, out_specs=out_specs, check_vma=False
    )
```

profile of v0, /device:TPU:8, one launch (start us, length us, event | category | flops | bytes accessed | tf_op | source)
XLA Modules:
  0.0 386.3 jit_solution(8638338468976449265)
XLA Ops:
  7.2 0.0 copy-start
  7.2 0.0 all-gather.5.cloned.1.call-start
  7.2 0.7 all-gather.5.cloned.1.call-update
  7.9 0.0 all-gather.3.cloned.1.call-start
  8.0 0.7 all-gather.3.cloned.1.call-update
  8.7 0.0 reduce-scatter.3.cloned.1.call-start
  8.7 1.3 fusion.33
  13.9 0.7 constant_dynamic-slice_fusion.2
  14.6 38.0 %all_gather.11 = bf16[32,32,128]{2,1,0:T(8,128)(2,1)S(1)} all-gather(bf16[1,32,128]{2,1,0:T(8,128)(2,1)S(1)} %constant_dynamic-slice_fusion.2), channel_id=1, replica_groups=mesh['blk'=32,'tp'=8] {'blk'}, dimensions={0}, use_global_device_ids=true | all-gather | bytes 270336 | tf_op jit(solution)/shard_map/all_gather | solution.py:23
  52.6 0.0 copy-done
  52.6 3.4 fusion.34
  56.1 8.7 %all-gather.5.cloned.1.call-done = bf16[256,2048]{1,0:T(8,128)(2,1)} async-done(((bf16[32,2048]{1,0:T(8,128)(2,1)}), bf16[256,2048]{1,0:T(8,128)(2,1)}) %all-gather.5.cloned.1.call-update) | async-done | bytes 1048592 | tf_op jit(solution)/shard_map/all_gather | solution.py:25
  64.8 0.0 copy-start.3
  64.8 1.0 fusion.7
  65.8 1.0 fusion.11
  66.8 63.7 %all-gather.3.cloned.1.call-done = bf16[32,1024,32]{1,2,0:T(8,128)(2,1)} async-done(((bf16[1,1024,32]{1,2,0:T(8,128)(2,1)}), bf16[32,1024,32]{1,2,0:T(8,128)(2,1)}) %all-gather.3.cloned.1.call-update) | async-done | bytes 2097168 | tf_op jit(solution)/shard_map/all_gather | solution.py:24
  130.4 0.9 constant_dynamic-slice_fusion.4
  131.3 0.3 convolution_bitcast_fusion.1
  131.6 36.5 %psum.7 = bf16[2,2,128,32]{2,3,1,0:T(8,128)(2,1)S(1)} all-reduce(f32[2,2,128,32]{2,3,1,0:T(8,128)S(1)} %pad_maximum_fusion.3), channel_id=1, replica_groups=mesh['blk'=32,'tp'=8] {'tp'}, use_global_device_ids=true, to_apply=%region_0.0 | all-reduce | flops 16384 | bytes 98304 | tf_op jit(solution)/shard_map/psum | solution.py:40
  168.2 0.2 convolution_multiply_fusion.2
  168.4 0.2 convolution_multiply_fusion.3
  168.7 0.0 copy-start.1
  168.7 1.4 copy-done.1
  170.1 0.0 reduce-scatter.3.cloned.1.call-update
  170.1 0.0 reduce-scatter.5.cloned.1.call-start
  170.2 1.0 fusion.9
  171.1 1.0 fusion.5
  172.2 0.2 fusion.1
  172.4 0.3 copy.12
  172.7 0.6 reshape.50
  173.3 0.0 copy-done.3
  173.3 2.2 convolution_bitcast_fusion
  175.5 3.0 copy.15
  178.4 0.0 copy-start.2
  178.4 0.0 reduce-scatter.5.cloned.1.call-update
  178.5 0.3 convolution_multiply_fusion
  178.8 0.8 copy-done.2
  179.7 4.3 %fusion = bf16[256,1024]{1,0:T(8,128)(2,1)} fusion(f32[256,1024]{1,0:T(8,128)S(1)} %bitcast.43, bf16[256,2048]{1,0:T(8,128)(2,1)S(1)} %copy-done.2, bf16[1024,2048]{1,0:T(8,128)(2,1)} %param.7), kind=kOutput, calls=%fused_computation.3 | convolution fusion | flops 1074266112 | bytes 6815744 | tf_op jit(solution)/shard_map/dot_general | solution.py:60
  183.9 67.5 %reduce-scatter.3.cloned.1.call-done = f32[32,2048]{1,0:T(8,128)} async-done(((f32[256,2048]{1,0:T(8,128)}), f32[32,2048]{1,0:T(8,128)}) %reduce-scatter.3.cloned.1.call-update) | async-done | bytes 262160 | tf_op jit(solution)/shard_map/reduce_scatter | solution.py:59
  251.5 1.6 convert_element_type.16
  253.1 123.1 %reduce-scatter.5.cloned.1.call-done = f32[1,288,128]{2,1,0:T(8,128)} async-done(((f32[32,288,128]{2,1,0:T(8,128)}), f32[1,288,128]{2,1,0:T(8,128)}) %reduce-scatter.5.cloned.1.call-update) | async-done | bytes 147472 | tf_op jit(solution)/shard_map/reduce_scatter | solution.py:82
  376.2 1.3 slice.57
  377.5 1.2 slice_reduce_fusion
  378.7 0.2 reshape.53
  378.9 0.8 copy.13
  (8 shorter events, 0.1 us)
Async XLA Ops:
  7.2 45.5 %copy-start = (bf16[256,1024]{1,0:T(8,128)(2,1)S(1)}, bf16[256,1024]{1,0:T(8,128)(2,1)}, u32[]{:S(2)}) copy-start(bf16[256,1024]{1,0:T(8,128)(2,1)} %param.6) | copy-start | bytes 1572868
  7.2 57.6 %all-gather.5.cloned.1.call-start = ((), (), s32[]{:S(2)}) async-start(), calls=%async_computation.3 | async-start | bytes 1179648 | tf_op jit(solution)/shard_map/all_gather | solution.py:25
  7.9 122.5 %all-gather.3.cloned.1.call-start = ((), (), s32[]{:S(2)}) async-start(), calls=%async_computation.2 | async-start | bytes 2162688 | tf_op jit(solution)/shard_map/all_gather | solution.py:24
  8.7 242.8 %reduce-scatter.3.cloned.1.call-start = ((), (), s32[]{:S(2)}) async-start(), calls=%async_computation.4 | async-start | bytes 2359296 | tf_op jit(solution)/shard_map/reduce_scatter | solution.py:59
  64.8 108.5 %copy-start.3 = (s32[2,1]{0,1:T(1,128)S(1)}, s32[2,1]{0,1:T(1,128)}, u32[]{:S(2)}) copy-start(s32[2,1]{0,1:T(1,128)} %param.10) | copy-start | bytes 28
  168.7 1.4 copy-start.1
  170.1 206.0 %reduce-scatter.5.cloned.1.call-start = ((), (), s32[]{:S(2)}) async-start(), calls=%async_computation.5 | async-start | bytes 4866048 | tf_op jit(solution)/shard_map/reduce_scatter | solution.py:82
  178.4 1.2 copy-start.2
Sparse Core Ops, SparseCore 0:
  10.7 54.0 all-gather.4
  66.7 63.7 all-gather.2
  170.2 81.1 reduce-scatter.2
  253.9 122.2 reduce-scatter.4
where the time goes:
time: 387 us; the launch traced here: 386 us
  waiting for transfers between devices  264 us (68%)
  blocking collectives  74.6 us (19%)
  between operations  17.8 us (5%)
  matrix products  15 us (4%)
  local copies, waits for them, and re-layouts  12.6 us (3%)
    reduce_scatter x1, waiting for transfers between devices, on_device(): lax.psum_scatter(dense.reshape(adapters, -1, 128), 'blk', scatter_dimensi...  123 us
    reduce_scatter x1, waiting for transfers between devices, on_device(): lax.psum_scatter(base, 'tp', scatter_dimension=0, tiled=True).astype(bf16)  67.5 us
    all_gather x1, waiting for transfers between devices, on_device(): all_a = lax.all_gather(bank_a, 'blk', axis=0, tiled=True)  63.7 us
    all_gather x1, blocking collectives, on_device(): all_b = lax.all_gather(b_cols, 'blk', axis=0, tiled=True)  38 us
    psum x1, blocking collectives, on_device(): both = lax.psum(jnp.stack([act_part, grad_part]), 'tp')  36.5 us
    all_gather x1, waiting for transfers between devices, on_device(): grad_rows = lax.all_gather(grad_out, 'tp', axis=0, tiled=True)  8.72 us
  transfers between devices with their start and end apart: 4, of which 4 were waited for; matrix products, arithmetic and copies ran while one was open for 6% of the time, Pallas kernels for 0%

commit v1 on v0

--- a/solution.py
+++ b/solution.py
@@ -22,7 +22,9 @@
     b_cols = lax.dynamic_slice_in_dim(bank_b, col0, kv_dev, 2)
     all_b = lax.all_gather(b_cols, "blk", axis=0, tiled=True)
     all_a = lax.all_gather(bank_a, "blk", axis=0, tiled=True)
-    grad_rows = lax.all_gather(grad_out, "tp", axis=0, tiled=True)
+    grad_rows = jnp.concatenate(
+        lax.all_to_all(jnp.stack([grad_out] * lax.axis_size("tp")), "tp", 0, 0), axis=0
+    )
     fac_a = jnp.stack([all_a[tile_ids[t]] for t in range(tiles)])
     fac_b = jnp.stack([all_b[tile_ids[t]] for t in range(tiles)])
     tok_t = tokens.reshape(tiles, tile_rows, feats)

time: 387 us -> 334 us (0.86)
  waiting for transfers between devices: 264 us -> 204 us
  starting transfers between devices: 0.16 us -> 7.46 us
    all_gather x1, waiting for transfers between devices: 63.7 us -> 11.8 us  [on_device(): all_a = lax.all_gather(bank_a, 'blk', axis=0, tiled=True)]
    all_gather x1 -> x0, waiting for transfers between devices: 8.72 us -> none  [on_device(): grad_rows = lax.all_gather(grad_out, 'tp', axis=0, tiled=True)]
    all_to_all x0 -> x1, starting transfers between devices: none -> 7.38 us  [on_device(): lax.all_to_all(jnp.stack([grad_out] * lax.axis_size('tp')), 'tp', 0, 0)]
  transfers between devices with their start and end apart: 4 -> 4, of which waited for: 4 -> 3; matrix products, arithmetic and copies ran while one was open for 6% -> 7% of each run, Pallas kernels for 0% -> 0%
where the time goes in v1:
time: 334 us; the launch traced here: 333 us
  waiting for transfers between devices  204 us (61%)
  blocking collectives  73.6 us (22%)
  between operations  17.8 us (5%)
  matrix products  15.4 us (5%)
  local copies, waits for them, and re-layouts  13.8 us (4%)
  starting transfers between devices  7.46 us (2%)
    reduce_scatter x1, waiting for transfers between devices, on_device(): lax.psum_scatter(dense.reshape(adapters, -1, 128), 'blk', scatter_dimensi...  123 us
    reduce_scatter x1, waiting for transfers between devices, on_device(): lax.psum_scatter(base, 'tp', scatter_dimension=0, tiled=True).astype(bf16)  68 us
    all_gather x1, blocking collectives, on_device(): all_b = lax.all_gather(b_cols, 'blk', axis=0, tiled=True)  37 us
    psum x1, blocking collectives, on_device(): both = lax.psum(jnp.stack([act_part, grad_part]), 'tp')  36.6 us
    all_gather x1, waiting for transfers between devices, on_device(): all_a = lax.all_gather(bank_a, 'blk', axis=0, tiled=True)  11.8 us
    all_to_all x1, starting transfers between devices, on_device(): lax.all_to_all(jnp.stack([grad_out] * lax.axis_size('tp')), 'tp', 0, 0)  7.38 us
  transfers between devices with their start and end apart: 4, of which 3 were waited for; matrix products, arithmetic and copies ran while one was open for 7% of the time, Pallas kernels for 0%

profile of v1, /device:TPU:8, one launch (start us, length us, event | category | flops | bytes accessed | tf_op | source)
XLA Modules:
  0.0 333.4 jit_solution(10787583234750047959)
XLA Ops:
  7.2 0.0 copy-start
  7.2 0.0 all-gather.2.cloned.1.call-start
  7.2 0.7 all-gather.2.cloned.1.call-update
  7.9 2.0 stack.28
  9.9 7.4 %all-to-all-start = ((bf16[8,32,2048]{2,1,0:T(8,128)(2,1)}), bf16[8,32,2048]{2,1,0:T(8,128)(2,1)}, u32[]{:S(2)}, u32[]{:S(2)}) async-start(bf16[8,32,2048]{2,1,0:T(8,128)(2,1)} %stack.28), calls=%async_computation | async-start | bytes 2097152 | tf_op jit(solution)/shard_map/all_to_all | solution.py:26
  17.3 0.0 reduce-scatter.3.cloned.1.call-start
  17.3 1.3 fusion.33
  22.5 0.7 constant_dynamic-slice_fusion.2
  23.2 37.0 %all_gather.7 = bf16[32,32,128]{2,1,0:T(8,128)(2,1)S(1)} all-gather(bf16[1,32,128]{2,1,0:T(8,128)(2,1)S(1)} %constant_dynamic-slice_fusion.2), channel_id=1, replica_groups=mesh['blk'=32,'tp'=8] {'blk'}, dimensions={0}, use_global_device_ids=true | all-gather | bytes 270336 | tf_op jit(solution)/shard_map/all_gather | solution.py:23
  60.2 0.0 copy-done
  60.2 3.5 %fusion.34 = f32[256,2048]{1,0:T(8,128)S(1)} fusion(bf16[256,1024]{1,0:T(8,128)(2,1)S(1)} %copy-done, bf16[1024,2048]{1,0:T(8,128)(2,1)} %param.7), kind=kOutput, calls=%fused_computation.59 | convolution fusion | flops 1073741824 | bytes 6815744 | tf_op jit(solution)/shard_map/dot_general | solution.py:51
  63.7 0.0 all-to-all-done
  63.7 0.0 copy-start.2
  63.7 1.0 fusion.7
  64.7 1.0 fusion.11
  65.7 11.8 %all-gather.2.cloned.1.call-done = bf16[32,1024,32]{1,2,0:T(8,128)(2,1)} async-done(((bf16[1,1024,32]{1,2,0:T(8,128)(2,1)}), bf16[32,1024,32]{1,2,0:T(8,128)(2,1)}) %all-gather.2.cloned.1.call-update) | async-done | bytes 2097168 | tf_op jit(solution)/shard_map/all_gather | solution.py:24
  77.5 0.9 constant_dynamic-slice_fusion.4
  78.4 0.3 convolution_bitcast_fusion.1
  78.7 36.6 %psum.7 = bf16[2,2,128,32]{2,3,1,0:T(8,128)(2,1)S(1)} all-reduce(f32[2,2,128,32]{2,3,1,0:T(8,128)S(1)} %pad_maximum_fusion.3), channel_id=1, replica_groups=mesh['blk'=32,'tp'=8] {'tp'}, use_global_device_ids=true, to_apply=%region_0.0 | all-reduce | flops 16384 | bytes 98304 | tf_op jit(solution)/shard_map/psum | solution.py:42
  115.3 0.2 convolution_multiply_fusion.2
  115.5 0.2 convolution_multiply_fusion.3
  115.8 0.0 copy-start.1
  115.8 1.4 copy-done.1
  117.2 0.0 reduce-scatter.3.cloned.1.call-update
  117.2 0.0 reduce-scatter.5.cloned.1.call-start
  117.2 1.0 fusion.9
  118.2 1.0 fusion.5
  119.2 0.2 fusion.1
  119.4 0.3 copy.12
  119.8 0.6 reshape.52
  120.4 0.0 copy-done.2
  120.4 2.1 convolution_bitcast_fusion
  122.5 3.0 copy.15
  125.5 0.0 reduce-scatter.5.cloned.1.call-update
  125.5 0.3 convolution_multiply_fusion
  125.9 4.6 %fusion = bf16[256,1024]{1,0:T(8,128)(2,1)} fusion(f32[256,1024]{1,0:T(8,128)S(1)} %bitcast.44, bf16[256,2048]{1,0:T(8,128)(2,1)} %bitcast.10, bf16[1024,2048]{1,0:T(8,128)(2,1)} %param.7), kind=kOutput, calls=%fused_computation.3 | convolution fusion | flops 1074266112 | bytes 6815744 | tf_op jit(solution)/shard_map/dot_general | solution.py:62
  130.5 68.0 %reduce-scatter.3.cloned.1.call-done = f32[32,2048]{1,0:T(8,128)} async-done(((f32[256,2048]{1,0:T(8,128)}), f32[32,2048]{1,0:T(8,128)}) %reduce-scatter.3.cloned.1.call-update) | async-done | bytes 262160 | tf_op jit(solution)/shard_map/reduce_scatter | solution.py:61
  198.5 1.6 convert_element_type.16
  200.1 123.2 %reduce-scatter.5.cloned.1.call-done = f32[1,288,128]{2,1,0:T(8,128)} async-done(((f32[32,288,128]{2,1,0:T(8,128)}), f32[1,288,128]{2,1,0:T(8,128)}) %reduce-scatter.5.cloned.1.call-update) | async-done | bytes 147472 | tf_op jit(solution)/shard_map/reduce_scatter | solution.py:84
  323.3 1.3 slice.57
  324.7 1.2 slice_reduce_fusion
  325.9 0.2 reshape.55
  326.1 0.8 copy.13
  (8 shorter events, 0.1 us)
Async XLA Ops:
  7.2 53.1 %copy-start = (bf16[256,1024]{1,0:T(8,128)(2,1)S(1)}, bf16[256,1024]{1,0:T(8,128)(2,1)}, u32[]{:S(2)}) copy-start(bf16[256,1024]{1,0:T(8,128)(2,1)} %param.6) | copy-start | bytes 1572868
  7.2 70.3 %all-gather.2.cloned.1.call-start = ((), (), s32[]{:S(2)}) async-start(), calls=%async_computation.3 | async-start | bytes 2162688 | tf_op jit(solution)/shard_map/all_gather | solution.py:24
  9.9 53.8 %all-to-all-start = ((bf16[8,32,2048]{2,1,0:T(8,128)(2,1)}), bf16[8,32,2048]{2,1,0:T(8,128)(2,1)}, u32[]{:S(2)}, u32[]{:S(2)}) async-start(bf16[8,32,2048]{2,1,0:T(8,128)(2,1)} %stack.28), calls=%async_computation | async-start | bytes 2097152 | tf_op jit(solution)/shard_map/all_to_all | solution.py:26
  17.3 181.2 %reduce-scatter.3.cloned.1.call-start = ((), (), s32[]{:S(2)}) async-start(), calls=%async_computation.4 | async-start | bytes 2359296 | tf_op jit(solution)/shard_map/reduce_scatter | solution.py:61
  63.7 56.6 %copy-start.2 = (s32[2,1]{0,1:T(1,128)S(1)}, s32[2,1]{0,1:T(1,128)}, u32[]{:S(2)}) copy-start(s32[2,1]{0,1:T(1,128)} %param.10) | copy-start | bytes 28
  115.8 1.4 copy-start.1
  117.2 206.1 %reduce-scatter.5.cloned.1.call-start = ((), (), s32[]{:S(2)}) async-start(), calls=%async_computation.5 | async-start | bytes 4866048 | tf_op jit(solution)/shard_map/reduce_scatter | solution.py:84
Sparse Core Ops, SparseCore 0:
  9.9 67.5 all-gather.1
  117.3 81.1 reduce-scatter.2
  201.0 122.2 reduce-scatter.4
